TPU v7x, 32 devices: a whole 2x2x4 slice. The times are simulated.
32 devices in a mesh: rows: 16 (over z, y, x), rep: 2 (over core).
Axes of the slice: x: 2, y: 2, z: 4, core: 2. Of those that a mesh axis runs over, the one named last changes fastest.
Arguments:
- grad_out: bfloat16 [2048, 1024], P('rows'), may hold values from -8 to 8
- w_self: bfloat16 [1024, 1024], replicated, may hold values from -0.1875 to 0.1875
- w_neigh: bfloat16 [1024, 1024], replicated, may hold values from -0.1875 to 0.1875
- adj_tiles: bfloat16 [16, 8, 128, 128], P('rows'), may hold values from -0.3125 to 0.3125
- tile_index: int32 [16, 8], P('rows'), may hold values from 0 to 15, as said below
- tile_count: int32 [16], P('rows'), may hold values from 4 to 8, as said below
- prompt_ids: int32 [2048], P('rows'), may hold values from 0 to 15
Outputs:
- input_grad: bfloat16 [2048, 1024], P('rows')
- prompt_grad: float32 [16, 1024], replicated
Inputs may be any that keep to these rules, and one draw needn't show every extreme that they name: `tile_index`: each row holds 8 different tile numbers; only the first tile_count entries of a row are used. `tile_count`: some destination tile uses all 8 slots.
All inputs are finite; a program needn't handle non-finite values.
Results may differ from a plain program's by a relative error of at most 0.0041.
Values may be sent and summed in bfloat16 or wider, within the bound.
A program may use at most 64 MiB of HBM per device.

v0:
```python
import math
import jax
import jax.numpy as jnp
from jax import lax
from jax.sharding import PartitionSpec as P

PROMPTS = 16


def shards(grad_out, w_self, w_neigh, adj_tiles, tile_index, tile_count, prompt_ids):
    rows_dev, width = grad_out.shape
    local_tiles, max_slots, tile_size, _ = adj_tiles.shape
    n_rows = lax.axis_size("rows")
    n_rep = lax.axis_size("rep")
    rep_index = lax.axis_index("rep")
    total_tiles = local_tiles * n_rows
    slot_ids = jnp.arange(max_slots)
    in_use = slot_ids[None, :] < tile_count[:, None]
    matches = (tile_index[:, :, None] == jnp.arange(total_tiles)[None, None, :]) & in_use[
        :, :, None
    ]
    present = jnp.any(matches, axis=1)
    slot_table = jnp.argmax(matches, axis=1)
    contract = (((1,), (1,)), ((), ()))
    half_rows = rows_dev // n_rep
    mine = lax.dynamic_slice_in_dim(grad_out, rep_index * half_rows, half_rows, 0)
    initial = jnp.zeros((local_tiles, tile_size, width), jnp.float32)

    def half_column(place):
        return place // half_rows * rows_dev + rep_index * half_rows + place % half_rows

    piece = lax.all_gather(mine, "rows", axis=0, tiled=True)
    piece_rows = piece.shape[0]
    unit = math.gcd(math.gcd(piece_rows, tile_size), half_rows)
    segments = piece_rows // unit
    feat = piece.shape[1]

    def one_segment(index, carry):
        start = index * unit
        rows_part = lax.dynamic_slice_in_dim(piece, start, unit, 0)
        column = half_column(start)
        source = column // tile_size
        offset = column % tile_size
        slot = slot_table[0, source]
        zero = jnp.zeros((), jnp.int32)
        block = lax.dynamic_slice(
            adj_tiles, (jnp.int32(0), slot, zero, offset), (1, 1, tile_size, unit)
        )
        block = block.reshape(tile_size, unit)

        def product(args):
            blk, part_rows = args
            return jnp.dot(blk, part_rows, preferred_element_type=jnp.float32)

        def nothing(args):
            return jnp.zeros((tile_size, feat), jnp.float32)

        term = lax.cond(present[0, source], product, nothing, (block, rows_part))
        updated = [carry[0] + term]
        return jnp.stack(updated, axis=0)

    partial_value = lax.fori_loop(0, segments, one_segment, initial)
    summed = lax.psum(partial_value.reshape(rows_dev, width), "rep")
    aggregate = summed.astype(jnp.bfloat16)
    full_grad = lax.dot_general(grad_out, w_self, contract, preferred_element_type=jnp.float32)
    full_grad = full_grad + lax.dot_general(
        aggregate, w_neigh, contract, preferred_element_type=jnp.float32
    )
    onehot = (prompt_ids[None, :] == jnp.arange(PROMPTS)[:, None]).astype(jnp.float32)
    prompt_part = jnp.dot(onehot, full_grad, precision=lax.Precision.HIGHEST)
    prompt_grad = lax.psum(prompt_part, "rows")
    return (full_grad.astype(jnp.bfloat16), prompt_grad)


def solution(mesh):
    placed = (
        P("rows", None),
        P(),
        P(),
        P("rows", None, None, None),
        P("rows", None),
        P("rows"),
        P("rows"),
    )
    return jax.shard_map(
        shards, mesh=mesh, in_specs=placed, out_specs=(P("rows", None), P()), check_vma=False
    )
```

profile of v0, /device:TPU:0, one launch (start us, length us, event | category | flops | bytes accessed | tf_op | source)
XLA Modules:
  0.0 249.7 jit_solution(9167569189331557641)
XLA Ops:
  7.2 1.7 constant_dynamic-slice_fusion.2
  9.7 0.7 fusion.10
  10.4 1.3 iota_reduce_fusion
  11.7 3.3 %fusion.13 = f32[128,1024]{1,0:T(8,128)} fusion(bf16[128,1024]{1,0:T(8,128)(2,1)} %param.11, bf16[1024,1024]{1,0:T(8,128)(2,1)} %param.12), kind=kOutput, calls=%fused_computation.22 | convolution fusion | flops 268435456 | bytes 2883584 | tf_op jit(solution)/shard_map/dot_general | solution.py:65
  15.0 59.5 %all-gather.2.cloned.1.call-done = bf16[1024,1024]{1,0:T(8,128)(2,1)} async-done(((bf16[64,1024]{1,0:T(8,128)(2,1)}), bf16[1024,1024]{1,0:T(8,128)(2,1)}) %all-gather.2.cloned.1.call-update) | async-done | bytes 2097168 | tf_op jit(solution)/shard_map/all_gather | solution.py:32
  74.5 45.9 %while.16 = (s32[]{:T(128)}, f32[1,128,1024]{2,1,0:T(8,128)S(1)}, s32[]{:T(128)}, pred[1,16]{1,0:T(4,128)(4,1)S(1)}, s32[1,16]{1,0:T(1,128)S(1)}, /*index=5*/bf1...) while((s32[]{:T(128)}, f32[1,128,1024]{2,1,0:T(8,128)S(1)}, ...), condition=%wide.region_5.6_spmd, body=%wide.region_2.5_spmd.sunk | while | flops 16908344 | bytes 2261804 | solution.py:62
  74.6 0.7 fusion.21
  75.3 4.7 %conditional.2 = (f32[128,1024]{1,0:T(8,128)S(1)}) conditional(s32[]{:T(128)} %bitcast.25, () %tuple.66, (s32[1,16]{1,0:T(1,128)S(1)}, s32[]{:T(128)}, s32[]{:T(128)}, bf16[1,8,128,128]{3,2,1,0:T(8,128)(2,1)}, s32[]{:T(128)}, /*index=5*/pred[]{:T(512)}, bf16[1024,1024]{1,0:T(8,128)(2,1)}) %tuple.67), branch_computations={%region_3.3_spmd, %region_4.4_spmd} | conditional | flops 16777228 | bytes 688299 | solution.py:58
  76.0 0.7 constant_dynamic-slice_fusion
  78.7 1.2 fusion
  79.9 0.1 fusion.22
  80.1 0.7 fusion.21
  80.8 4.7 %conditional.2 = (f32[128,1024]{1,0:T(8,128)S(1)}) conditional(s32[]{:T(128)} %bitcast.25, () %tuple.66, (s32[1,16]{1,0:T(1,128)S(1)}, s32[]{:T(128)}, s32[]{:T(128)}, bf16[1,8,128,128]{3,2,1,0:T(8,128)(2,1)}, s32[]{:T(128)}, /*index=5*/pred[]{:T(512)}, bf16[1024,1024]{1,0:T(8,128)(2,1)}) %tuple.67), branch_computations={%region_3.3_spmd, %region_4.4_spmd} | conditional | flops 16777228 | bytes 688299 | solution.py:58
  81.5 0.7 constant_dynamic-slice_fusion
  84.3 1.2 fusion
  85.7 0.7 fusion.21
  86.4 0.8 conditional.2
  87.1 0.1 fusion.22
  87.3 0.7 fusion.21
  88.0 0.8 conditional.2
  88.8 0.1 fusion.22
  89.0 0.7 fusion.21
  89.7 0.8 conditional.2
  90.4 0.1 fusion.22
  90.6 0.7 fusion.21
  91.3 4.7 %conditional.2 = (f32[128,1024]{1,0:T(8,128)S(1)}) conditional(s32[]{:T(128)} %bitcast.25, () %tuple.66, (s32[1,16]{1,0:T(1,128)S(1)}, s32[]{:T(128)}, s32[]{:T(128)}, bf16[1,8,128,128]{3,2,1,0:T(8,128)(2,1)}, s32[]{:T(128)}, /*index=5*/pred[]{:T(512)}, bf16[1024,1024]{1,0:T(8,128)(2,1)}) %tuple.67), branch_computations={%region_3.3_spmd, %region_4.4_spmd} | conditional | flops 16777228 | bytes 688299 | solution.py:58
  92.0 0.7 constant_dynamic-slice_fusion
  94.8 1.2 fusion
  96.0 0.1 fusion.22
  96.2 0.7 fusion.21
  96.9 4.7 %conditional.2 = (f32[128,1024]{1,0:T(8,128)S(1)}) conditional(s32[]{:T(128)} %bitcast.25, () %tuple.66, (s32[1,16]{1,0:T(1,128)S(1)}, s32[]{:T(128)}, s32[]{:T(128)}, bf16[1,8,128,128]{3,2,1,0:T(8,128)(2,1)}, s32[]{:T(128)}, /*index=5*/pred[]{:T(512)}, bf16[1024,1024]{1,0:T(8,128)(2,1)}) %tuple.67), branch_computations={%region_3.3_spmd, %region_4.4_spmd} | conditional | flops 16777228 | bytes 688299 | solution.py:58
  97.6 0.7 constant_dynamic-slice_fusion
  100.3 1.2 fusion
  101.5 0.1 fusion.22
  101.8 0.7 fusion.21
  102.4 0.8 conditional.2
  103.2 0.1 fusion.22
  103.4 0.7 fusion.21
  104.1 0.8 conditional.2
  104.8 0.1 fusion.22
  105.0 0.7 fusion.21
  105.7 0.8 conditional.2
  106.5 0.1 fusion.22
  106.7 0.7 fusion.21
  107.3 4.7 %conditional.2 = (f32[128,1024]{1,0:T(8,128)S(1)}) conditional(s32[]{:T(128)} %bitcast.25, () %tuple.66, (s32[1,16]{1,0:T(1,128)S(1)}, s32[]{:T(128)}, s32[]{:T(128)}, bf16[1,8,128,128]{3,2,1,0:T(8,128)(2,1)}, s32[]{:T(128)}, /*index=5*/pred[]{:T(512)}, bf16[1024,1024]{1,0:T(8,128)(2,1)}) %tuple.67), branch_computations={%region_3.3_spmd, %region_4.4_spmd} | conditional | flops 16777228 | bytes 688299 | solution.py:58
  108.1 0.7 constant_dynamic-slice_fusion
  110.8 1.2 fusion
  112.0 0.1 fusion.22
  112.2 0.7 fusion.21
  112.9 0.8 conditional.2
  113.7 0.1 fusion.22
  113.9 0.7 fusion.21
  114.5 0.8 conditional.2
  115.5 0.7 fusion.21
  116.2 0.8 conditional.2
  117.2 0.7 fusion.21
  117.8 0.8 conditional.2
  118.8 0.7 fusion.21
  119.5 0.8 conditional.2
  120.4 4.8 %all-reduce.4 = bf16[128,1024]{1,0:T(8,128)(2,1)S(1)} all-reduce(f32[128,1024]{1,0:T(8,128)S(1)} %bitcast.27), channel_id=1, replica_groups=mesh['rows'=16,'rep'=2] {'rep'}, use_global_device_ids=true, to_apply=%region_6.7 | all-reduce | flops 131072 | bytes 786432 | tf_op jit(solution)/shard_map/psum | solution.py:63
  125.2 2.6 %fusion.12 = (bf16[128,1024]{1,0:T(8,128)(2,1)}, f32[128,1024]{1,0:T(8,128)S(1)}) fusion(f32[128,1024]{1,0:T(8,128)} %fusion.13, bf16[128,1024]{1,0:T(8,128)(2,1)S(1)} %all-reduce.4, bf16[1024,1024]{1,0:T(8,128)(2,1)S(1)} %copy-done), kind=kOutput, calls=%fused_computation.21 | convolution fusion | flops 268697600 | bytes 3670016 | tf_op jit(solution)/shard_map/dot_general | solution.py:66
  127.8 0.9 fusion.7
  128.8 112.6 %all-reduce.3.cloned.1.call-done = f32[16,1024]{1,0:T(8,128)} async-done(((f32[16,1024]{1,0:T(8,128)}), f32[16,1024]{1,0:T(8,128)}) %all-reduce.3.cloned.1.call-update) | async-done | bytes 65552 | tf_op jit(solution)/shard_map/psum | solution.py:71
  241.4 1.5 copy.21
  (26 shorter events, 1.3 us)
Async XLA Ops:
  7.2 118.1 %copy-start = (bf16[1024,1024]{1,0:T(8,128)(2,1)S(1)}, bf16[1024,1024]{1,0:T(8,128)(2,1)}, u32[]{:S(2)}) copy-start(bf16[1024,1024]{1,0:T(8,128)(2,1)} %param.13) | copy-start | bytes 6291460
  7.2 67.3 %all-gather.2.cloned.1.call-start = ((), (), s32[]{:S(2)}) async-start(), calls=%async_computation | async-start | bytes 2228224 | tf_op jit(solution)/shard_map/all_gather | solution.py:32
  9.0 232.4 %all-reduce.3.cloned.1.call-start = ((), (), s32[]{:S(2)}) async-start(), calls=%async_computation.1 | async-start | bytes 131072 | tf_op jit(solution)/shard_map/psum | solution.py:71
  120.4 7.4 %copy-start.1 = (s32[128]{0:T(128)S(1)}, s32[128]{0:T(128)}, u32[]{:S(2)}) copy-start(s32[128]{0:T(128)} %param.17) | copy-start | bytes 1540
Sparse Core Ops, SparseCore 0:
  11.3 63.0 all-gather.1
  128.9 112.4 all-reduce.2
where the time goes:
time: 250 us
  waiting for transfers between devices  172 us (69%)
  loops' own time  23.3 us (9%)
  other arithmetic  14.8 us (6%)
  between operations  14.7 us (6%)
  matrix products  12.8 us (5%)
  local copies, waits for them, and re-layouts  7.06 us (3%)
  blocking collectives  4.82 us (2%)
    psum x1, waiting for transfers between devices, shards(): prompt_grad = lax.psum(prompt_part, 'rows')  113 us
    all_gather x1, waiting for transfers between devices, shards(): piece = lax.all_gather(mine, 'rows', axis=0, tiled=True)  59.5 us
    another operation x16, loops' own time, one_segment(): term = lax.cond(present[0, source], product, nothing, (block, rows_part))  21.9 us
    convert_element_type x16, other arithmetic, one_segment(): term = lax.cond(present[0, source], product, nothing, (block, rows_part))  10.6 us
    dot_general x5, matrix products, product(): return jnp.dot(blk, part_rows, preferred_element_type=jnp.float32)  5.96 us
  transfers between devices with their start and end apart: 2, of which 2 were waited for; matrix products, arithmetic and copies ran while one was open for 2% of the time, Pallas kernels for 0%

commit v1 on v0

--- a/solution.py
+++ b/solution.py
@@ -68,7 +68,7 @@
     )
     onehot = (prompt_ids[None, :] == jnp.arange(PROMPTS)[:, None]).astype(jnp.float32)
     prompt_part = jnp.dot(onehot, full_grad, precision=lax.Precision.HIGHEST)
-    prompt_grad = lax.psum(prompt_part, "rows")
+    prompt_grad = jnp.sum(lax.all_gather(prompt_part, "rows"), axis=0)
     return (full_grad.astype(jnp.bfloat16), prompt_grad)
 
 

time: 250 us -> 203 us (0.81)
  waiting for transfers between devices: 172 us -> 124 us
    psum x1 -> x0, waiting for transfers between devices: 113 us -> none  [shards(): prompt_grad = lax.psum(prompt_part, 'rows')]
    all_gather x0 -> x1, waiting for transfers between devices: none -> 64.2 us  [shards(): prompt_grad = jnp.sum(lax.all_gather(prompt_part, 'rows'), axis=0)]
  transfers between devices with their start and end apart: 2 -> 2, of which waited for: 2 -> 2; matrix products, arithmetic and copies ran while one was open for 2% -> 3% of each run, Pallas kernels for 0% -> 0%
where the time goes in v1:
time: 203 us; the launch traced here: 202 us
  waiting for transfers between devices  124 us (61%)
  loops' own time  23.3 us (11%)
  other arithmetic  16.7 us (8%)
  between operations  14.7 us (7%)
  matrix products  12.8 us (6%)
  local copies, waits for them, and re-layouts  5.59 us (3%)
  blocking collectives  4.82 us (2%)
    all_gather x1, waiting for transfers between devices, shards(): prompt_grad = jnp.sum(lax.all_gather(prompt_part, 'rows'), axis=0)  64.2 us
    all_gather x1, waiting for transfers between devices, shards(): piece = lax.all_gather(mine, 'rows', axis=0, tiled=True)  59.5 us
    another operation x16, loops' own time, one_segment(): term = lax.cond(present[0, source], product, nothing, (block, rows_part))  21.9 us
    convert_element_type x16, other arithmetic, one_segment(): term = lax.cond(present[0, source], product, nothing, (block, rows_part))  10.6 us
    dot_general x5, matrix products, product(): return jnp.dot(blk, part_rows, preferred_element_type=jnp.float32)  5.96 us
    psum x1, blocking collectives, shards(): summed = lax.psum(partial_value.reshape(rows_dev, width), 'rep')  4.82 us
  transfers between devices with their start and end apart: 2, of which 2 were waited for; matrix products, arithmetic and copies ran while one was open for 3% of the time, Pallas kernels for 0%

profile of v1, /device:TPU:0, one launch (start us, length us, event | category | flops | bytes accessed | tf_op | source)
XLA Modules:
  0.0 201.8 jit_solution(6527669584327510367)
XLA Ops:
  7.2 1.7 constant_dynamic-slice_fusion.2
  9.7 0.7 fusion.10
  10.4 1.3 iota_reduce_fusion
  11.7 3.3 %fusion.13 = f32[128,1024]{1,0:T(8,128)} fusion(bf16[128,1024]{1,0:T(8,128)(2,1)} %param.11, bf16[1024,1024]{1,0:T(8,128)(2,1)} %param.12), kind=kOutput, calls=%fused_computation.22 | convolution fusion | flops 268435456 | bytes 2883584 | tf_op jit(solution)/shard_map/dot_general | solution.py:65
  15.0 59.5 %all-gather.4.cloned.1.call-done = bf16[1024,1024]{1,0:T(8,128)(2,1)} async-done(((bf16[64,1024]{1,0:T(8,128)(2,1)}), bf16[1024,1024]{1,0:T(8,128)(2,1)}) %all-gather.4.cloned.1.call-update) | async-done | bytes 2097168 | tf_op jit(solution)/shard_map/all_gather | solution.py:32
  74.5 45.9 %while.16 = (s32[]{:T(128)}, f32[1,128,1024]{2,1,0:T(8,128)S(1)}, s32[]{:T(128)}, pred[1,16]{1,0:T(4,128)(4,1)S(1)}, s32[1,16]{1,0:T(1,128)S(1)}, /*index=5*/bf1...) while((s32[]{:T(128)}, f32[1,128,1024]{2,1,0:T(8,128)S(1)}, ...), condition=%wide.region_5.6_spmd, body=%wide.region_2.5_spmd.sunk | while | flops 16908344 | bytes 2261804 | solution.py:62
  74.6 0.7 fusion.21
  75.3 4.7 %conditional.2 = (f32[128,1024]{1,0:T(8,128)S(1)}) conditional(s32[]{:T(128)} %bitcast.26, () %tuple.66, (s32[1,16]{1,0:T(1,128)S(1)}, s32[]{:T(128)}, s32[]{:T(128)}, bf16[1,8,128,128]{3,2,1,0:T(8,128)(2,1)}, s32[]{:T(128)}, /*index=5*/pred[]{:T(512)}, bf16[1024,1024]{1,0:T(8,128)(2,1)}) %tuple.67), branch_computations={%region_3.3_spmd, %region_4.4_spmd} | conditional | flops 16777228 | bytes 688299 | solution.py:58
  76.0 0.7 constant_dynamic-slice_fusion
  78.7 1.2 fusion
  79.9 0.1 fusion.22
  80.1 0.7 fusion.21
  80.8 4.7 %conditional.2 = (f32[128,1024]{1,0:T(8,128)S(1)}) conditional(s32[]{:T(128)} %bitcast.26, () %tuple.66, (s32[1,16]{1,0:T(1,128)S(1)}, s32[]{:T(128)}, s32[]{:T(128)}, bf16[1,8,128,128]{3,2,1,0:T(8,128)(2,1)}, s32[]{:T(128)}, /*index=5*/pred[]{:T(512)}, bf16[1024,1024]{1,0:T(8,128)(2,1)}) %tuple.67), branch_computations={%region_3.3_spmd, %region_4.4_spmd} | conditional | flops 16777228 | bytes 688299 | solution.py:58
  81.5 0.7 constant_dynamic-slice_fusion
  84.3 1.2 fusion
  85.7 0.7 fusion.21
  86.4 0.8 conditional.2
  87.1 0.1 fusion.22
  87.3 0.7 fusion.21
  88.0 0.8 conditional.2
  88.8 0.1 fusion.22
  89.0 0.7 fusion.21
  89.7 0.8 conditional.2
  90.4 0.1 fusion.22
  90.6 0.7 fusion.21
  91.3 4.7 %conditional.2 = (f32[128,1024]{1,0:T(8,128)S(1)}) conditional(s32[]{:T(128)} %bitcast.26, () %tuple.66, (s32[1,16]{1,0:T(1,128)S(1)}, s32[]{:T(128)}, s32[]{:T(128)}, bf16[1,8,128,128]{3,2,1,0:T(8,128)(2,1)}, s32[]{:T(128)}, /*index=5*/pred[]{:T(512)}, bf16[1024,1024]{1,0:T(8,128)(2,1)}) %tuple.67), branch_computations={%region_3.3_spmd, %region_4.4_spmd} | conditional | flops 16777228 | bytes 688299 | solution.py:58
  92.0 0.7 constant_dynamic-slice_fusion
  94.8 1.2 fusion
  96.0 0.1 fusion.22
  96.2 0.7 fusion.21
  96.9 4.7 %conditional.2 = (f32[128,1024]{1,0:T(8,128)S(1)}) conditional(s32[]{:T(128)} %bitcast.26, () %tuple.66, (s32[1,16]{1,0:T(1,128)S(1)}, s32[]{:T(128)}, s32[]{:T(128)}, bf16[1,8,128,128]{3,2,1,0:T(8,128)(2,1)}, s32[]{:T(128)}, /*index=5*/pred[]{:T(512)}, bf16[1024,1024]{1,0:T(8,128)(2,1)}) %tuple.67), branch_computations={%region_3.3_spmd, %region_4.4_spmd} | conditional | flops 16777228 | bytes 688299 | solution.py:58
  97.6 0.7 constant_dynamic-slice_fusion
  100.3 1.2 fusion
  101.5 0.1 fusion.22
  101.8 0.7 fusion.21
  102.4 0.8 conditional.2
  103.2 0.1 fusion.22
  103.4 0.7 fusion.21
  104.1 0.8 conditional.2
  104.8 0.1 fusion.22
  105.0 0.7 fusion.21
  105.7 0.8 conditional.2
  106.5 0.1 fusion.22
  106.7 0.7 fusion.21
  107.3 4.7 %conditional.2 = (f32[128,1024]{1,0:T(8,128)S(1)}) conditional(s32[]{:T(128)} %bitcast.26, () %tuple.66, (s32[1,16]{1,0:T(1,128)S(1)}, s32[]{:T(128)}, s32[]{:T(128)}, bf16[1,8,128,128]{3,2,1,0:T(8,128)(2,1)}, s32[]{:T(128)}, /*index=5*/pred[]{:T(512)}, bf16[1024,1024]{1,0:T(8,128)(2,1)}) %tuple.67), branch_computations={%region_3.3_spmd, %region_4.4_spmd} | conditional | flops 16777228 | bytes 688299 | solution.py:58
  108.1 0.7 constant_dynamic-slice_fusion
  110.8 1.2 fusion
  112.0 0.1 fusion.22
  112.2 0.7 fusion.21
  112.9 0.8 conditional.2
  113.7 0.1 fusion.22
  113.9 0.7 fusion.21
  114.5 0.8 conditional.2
  115.5 0.7 fusion.21
  116.2 0.8 conditional.2
  117.2 0.7 fusion.21
  117.8 0.8 conditional.2
  118.8 0.7 fusion.21
  119.5 0.8 conditional.2
  120.4 4.8 %all-reduce.1 = bf16[128,1024]{1,0:T(8,128)(2,1)S(1)} all-reduce(f32[128,1024]{1,0:T(8,128)S(1)} %bitcast.28), channel_id=1, replica_groups=mesh['rows'=16,'rep'=2] {'rep'}, use_global_device_ids=true, to_apply=%region_6.7 | all-reduce | flops 131072 | bytes 786432 | tf_op jit(solution)/shard_map/psum | solution.py:63
  125.2 2.6 %fusion.12 = (bf16[128,1024]{1,0:T(8,128)(2,1)}, f32[128,1024]{1,0:T(8,128)S(1)}) fusion(f32[128,1024]{1,0:T(8,128)} %fusion.13, bf16[128,1024]{1,0:T(8,128)(2,1)S(1)} %all-reduce.1, bf16[1024,1024]{1,0:T(8,128)(2,1)S(1)} %copy-done), kind=kOutput, calls=%fused_computation.21 | convolution fusion | flops 268697600 | bytes 3670016 | tf_op jit(solution)/shard_map/dot_general | solution.py:66
  127.8 0.9 fusion.7
  128.8 64.2 %all-gather.6.cloned.1.call-done = f32[256,1024]{1,0:T(8,128)} async-done(((f32[16,1024]{1,0:T(8,128)}), f32[256,1024]{1,0:T(8,128)}) %all-gather.6.cloned.1.call-update) | async-done | bytes 1048592 | tf_op jit(solution)/shard_map/all_gather | solution.py:71
  193.0 1.9 reduce_sum.9
  (26 shorter events, 1.3 us)
Async XLA Ops:
  7.2 118.1 %copy-start = (bf16[1024,1024]{1,0:T(8,128)(2,1)S(1)}, bf16[1024,1024]{1,0:T(8,128)(2,1)}, u32[]{:S(2)}) copy-start(bf16[1024,1024]{1,0:T(8,128)(2,1)} %param.13) | copy-start | bytes 6291460
  7.2 67.3 %all-gather.4.cloned.1.call-start = ((), (), s32[]{:S(2)}) async-start(), calls=%async_computation | async-start | bytes 2228224 | tf_op jit(solution)/shard_map/all_gather | solution.py:32
  9.0 184.0 %all-gather.6.cloned.1.call-start = ((), (), s32[]{:S(2)}) async-start(), calls=%async_computation.1 | async-start | bytes 1114112 | tf_op jit(solution)/shard_map/all_gather | solution.py:71
  120.4 7.4 %copy-start.1 = (s32[128]{0:T(128)S(1)}, s32[128]{0:T(128)}, u32[]{:S(2)}) copy-start(s32[128]{0:T(128)} %param.17) | copy-start | bytes 1540
Sparse Core Ops, SparseCore 0:
  11.3 63.0 all-gather.3
  128.9 64.0 all-gather.5
